TPU v7x, 32 devices: a whole 2x2x4 slice. The times are simulated.
32 devices in a mesh: parts: 2 (over x), harm: 4 (over y, core), tile: 4 (over z).
Axes of the slice: x: 2, y: 2, z: 4, core: 2. Of those that a mesh axis runs over, the one named last changes fastest.
Arguments:
- perturbation: float32 [8, 2, 5, 128, 256], P('harm', None, None, ('parts', 'tile')), parts along dimension 3, may hold values from -6 to 6
- base_flow: float32 [8, 2, 3, 128, 256], P('harm', None, None, ('parts', 'tile')), parts along dimension 3, may hold values from -0.9 to 0.9
- viscosity: float32 [128, 256], P(('parts', 'tile')), parts along dimension 0, may hold values from 0.05 to 0.5
Outputs:
- resolvent_image: float32 [8, 2, 5, 128, 256], P('harm', None, None, ('parts', 'tile')), parts along dimension 3
There are 2 independent parts, one for each index of `parts`. A program takes and returns all parts, laid end to end along the dimension named above; each array names one. Nothing has to cross between parts.
All inputs are finite; a program needn't handle non-finite values.
Results may differ from a plain program's by a relative error of at most 0.00002.
Values sent between devices are 32-bit elements; how exact they have to be, the bound alone decides.
A program may use at most 64 MiB of HBM per device.

v0:
```python
import jax
import jax.numpy as jnp
import numpy as np
from jax import lax
from jax.sharding import PartitionSpec as P

omega_base = 0.25


def extended(cells, sides, width):
    for axis, dim in sides:
        count = lax.axis_size(axis)
        head = lax.slice_in_dim(cells, 0, width, axis=dim)
        tail = lax.slice_in_dim(cells, cells.shape[dim] - width, cells.shape[dim], axis=dim)
        cells = jnp.concatenate(
            [
                lax.ppermute(tail, axis, [(i, (i + 1) % count) for i in range(count)]),
                cells,
                lax.ppermute(head, axis, [((i + 1) % count, i) for i in range(count)]),
            ],
            axis=dim,
        )
    return cells


def shifted(value, axis, steps):
    count = lax.axis_size(axis)
    pairs = [(source, (source + steps) % count) for source in range(count)]
    return lax.ppermute(value, axis, pairs)


def split_rows(padded):
    middle = padded[..., 1:-1, :]
    grad_x = 0.5 * (padded[..., 2:, :] - padded[..., :-2, :])
    grad_y = 0.5 * (jnp.roll(middle, -1, -1) - jnp.roll(middle, 1, -1))
    return (middle, grad_x, grad_y)


def diffusion(padded, visc_padded):
    middle = padded[..., 1:-1, :]
    center = visc_padded[1:-1]
    east_face = 0.5 * (center + visc_padded[2:])
    west_face = 0.5 * (center + visc_padded[:-2])
    north_face = 0.5 * (center + jnp.roll(center, -1, -1))
    south_face = 0.5 * (center + jnp.roll(center, 1, -1))
    return (
        east_face * (padded[..., 2:, :] - middle)
        - west_face * (middle - padded[..., :-2, :])
        + north_face * (jnp.roll(middle, -1, -1) - middle)
        - south_face * (middle - jnp.roll(middle, 1, -1))
    )


def acoustic(grad_x, grad_y):
    dilation = grad_x[..., 1, :, :] + grad_y[..., 2, :, :]
    return jnp.stack(
        [dilation, grad_x[..., 4, :, :], grad_y[..., 4, :, :], jnp.zeros_like(dilation), dilation],
        axis=-3,
    )


def own_terms(middle, grad_x, grad_y, damping, frequency):
    rotation = jnp.stack([-frequency * middle[:, 1], frequency * middle[:, 0]], axis=1)
    return rotation + acoustic(grad_x, grad_y) - damping


def coupling(
    u_real, u_imag, v_real, v_imag, g_real, g_imag, q_real, q_imag, x_real, x_imag, y_real, y_imag
):
    real_part = (
        u_real * x_real
        - u_imag * x_imag
        + v_real * y_real
        - v_imag * y_imag
        + g_real * q_real
        - g_imag * q_imag
    )
    imag_part = (
        u_real * x_imag
        + u_imag * x_real
        + v_real * y_imag
        + v_imag * y_real
        + g_real * q_imag
        + g_imag * q_real
    )
    return (real_part, imag_part)


def block_terms(blocks, middle, grad_x, grad_y):
    local_count = middle.shape[0]
    index_table = np.array(
        [
            [local_count + target - source for source in range(local_count)]
            for target in range(local_count)
        ],
        dtype=np.int32,
    )
    chosen = blocks[index_table]

    def base_part(complex_index, field_index):
        return chosen[:, :, complex_index, field_index][:, :, None]

    def moved_part(values, complex_index):
        return values[None, :, complex_index]

    real_part, imag_part = coupling(
        base_part(0, 0),
        base_part(1, 0),
        base_part(0, 1),
        base_part(1, 1),
        base_part(0, 2),
        base_part(1, 2),
        moved_part(middle, 0),
        moved_part(middle, 1),
        moved_part(grad_x, 0),
        moved_part(grad_x, 1),
        moved_part(grad_y, 0),
        moved_part(grad_y, 1),
    )
    return jnp.stack([jnp.sum(real_part, axis=1), jnp.sum(imag_part, axis=1)], axis=1)


def shards(perturbation, base_flow, viscosity):
    local_count = perturbation.shape[0]
    width_x = perturbation.shape[3]
    width_y = perturbation.shape[4]
    groups = lax.axis_size("harm")
    first_index = lax.axis_index("harm") * local_count
    flattened = perturbation.reshape(local_count * 10, width_x, width_y)
    stacked = jnp.concatenate([flattened, viscosity[None]], axis=0)
    padded = extended(stacked, (("tile", 1),), 1)
    own_padded = padded[:-1].reshape(local_count, 2, 5, width_x + 2, width_y)
    visc_padded = padded[-1]
    numbers = first_index + jnp.arange(local_count, dtype=jnp.int32)
    total_count = local_count * groups
    signed = jnp.where(numbers < total_count // 2, numbers, numbers - total_count)
    frequency = (omega_base * signed.astype(jnp.float32)).reshape(local_count, 1, 1, 1)
    middle, grad_x, grad_y = split_rows(own_padded)
    summed = own_terms(middle, grad_x, grad_y, diffusion(own_padded, visc_padded), frequency)
    whole_base = lax.all_gather(base_flow, "harm", axis=0, tiled=True)

    def base_pair(position, earlier):
        before = lax.dynamic_slice_in_dim(
            whole_base, (position + groups - 1) % groups * local_count, local_count, 0
        )
        current = lax.dynamic_slice_in_dim(whole_base, position * local_count, local_count, 0)
        return (jnp.concatenate([before, current], axis=0), earlier)

    earlier = base_flow
    moving = own_padded

    def advance(moving):
        moved = shifted(moving, "harm", 1)
        return (moved, moved)

    blocks, earlier = base_pair(0, earlier)
    summed = summed + block_terms(blocks, middle, grad_x, grad_y)

    def advance_step(position, carried):
        summed, moving, earlier = carried
        moving, rimmed = advance(moving)
        blocks, earlier = base_pair(position, earlier)
        values, slope_x, slope_y = split_rows(rimmed)
        return (summed + block_terms(blocks, values, slope_x, slope_y), moving, earlier)

    summed, moving, earlier = lax.fori_loop(1, groups, advance_step, (summed, moving, earlier))
    return summed


def solution(mesh):
    placed = (
        P("harm", None, None, ("parts", "tile"), None),
        P("harm", None, None, ("parts", "tile"), None),
        P(("parts", "tile"), None),
    )
    return jax.shard_map(
        shards,
        mesh=mesh,
        in_specs=placed,
        out_specs=P("harm", None, None, ("parts", "tile"), None),
        check_vma=False,
    )
```

profile of v0, /device:TPU:0, one launch (start us, length us, event | category | flops | bytes accessed | tf_op | source)
XLA Modules:
  0.0 47.7 jit_solution(18082950959541213090)
XLA Ops:
  0.0 1.1 %pad_maximum_fusion.8 = (f32[21,1,256]{2,1,0:T(1,128)S(1)}, f32[21,1,256]{2,1,0:T(1,128)S(1)}) fusion(f32[1,16,256]{2,1,0:T(8,128)} %bitcast.94, f32[20,16,256]{2,1,0:T(8,128)} %bitcast.90), kind=kLoop, calls=%fused_computation.57 | loop fusion | flops 10752 | bytes 387072 | tf_op jit(solution)/shard_map/slice | solution.py:14
  1.1 5.1 %collective-permute-start.2 = (f32[21,1,256]{2,1,0:T(1,128)S(1)}, f32[21,1,256]{2,1,0:T(1,128)S(1)}, u32[]{:S(2)}, u32[]{:S(2)}) collective-permute-start(f32[21,1,256]{2,1,0:T(1,128)S(1)} %get-tuple-element.304), channel_id=1, source_target_pairs={{1,0},{2,1},{3,2},{0,3},{5,4},{6,5},{7,6},{4,7},{9,8},{10,9},{11,1... | collective-permute-start | bytes 64520 | tf_op jit(solution)/shard_map/ppermute | solution.py:19
  6.4 8.6 %all_gather.3 = f32[8,2,3,16,256]{4,3,2,1,0:T(8,128)S(1)} all-gather(f32[2,2,3,16,256]{4,3,2,1,0:T(8,128)S(1)} %copy-done.2), channel_id=1, replica_groups=mesh['parts'=2,'harm'=4,'tile'=4] {'harm'}, dimensions={0}, use_global_device_ids=true | all-gather | bytes 983040 | tf_op jit(solution)/shard_map/all_gather | solution.py:140
  15.0 0.6 %copy-done.3 = s32[4]{0:T(128)S(1)} copy-done((s32[4]{0:T(128)S(1)}, s32[4]{0:T(128)}, u32[]{:S(2)}) %copy-start.3) | copy-done | bytes 40
  15.7 0.6 %gather_fusion.1 = f32[4,2,3,16,256]{4,3,2,1,0:T(8,128)S(1)} fusion(f32[4,2,3,16,256]{4,3,2,1,0:T(8,128)S(1)} %pad_maximum_fusion.4, s32[1024]{0:T(1024)S(1)} %pad_clamp_fusion.1), kind=kCustom, calls=%fused_computation.1 | custom fusion | bytes 786448 | tf_op jit(solution)/shard_map/gather | solution.py:98
  16.4 0.9 %copy-done = f32[2,2,5,16,256]{4,3,2,1,0:T(8,128)S(1)} copy-done((f32[2,2,5,16,256]{4,3,2,1,0:T(8,128)S(1)}, f32[2,2,5,16,256]{4,3,2,1,0:T(8,128)}, u32[]{:S(2)}) %copy-start) | copy-done | bytes 327704
  17.6 0.2 subtract_multiply_fusion
  18.1 0.3 subtract_reduce_fusion.1
  18.5 0.3 fusion.3
  18.8 28.2 %while.21 = (s32[]{:T(128)}, f32[2,2,5,16,256]{4,3,2,0,1:T(8,128)S(1)}, f32[2,2,5,18,256]{4,3,2,0,1:T(8,128)S(1)}, f32[8,2,3,16,256]{4,3,2,1,0:T(8,128)S(1)}, s3...) while((s32[]{:T(128)}, ...), condition=%wide.region_5.6_spmd.clone, body=%wide.region_2.5_spmd.sunk.clone.sunk | while | flops 2638870 | bytes 13291922 | solution.py:166
  18.8 0.4 collective-permute-start
  19.3 0.6 %gather_fusion = f32[4,2,3,16,256]{4,3,2,1,0:T(8,128)S(1)} fusion(f32[4,2,3,16,256]{4,3,2,1,0:T(8,128)S(1)} %pad_maximum_fusion.14, s32[1024]{0:T(1024)S(1)} %pad_clamp_fusion.3), kind=kCustom, calls=%fused_computation.clone.1 | custom fusion | bytes 786448 | tf_op jit(solution)/shard_map/while/body/eval_jaxpr/gather | solution.py:98
  19.9 7.2 %collective-permute-done = f32[2,2,5,18,256]{4,3,2,0,1:T(8,128)S(1)} collective-permute-done((f32[2,2,5,18,256]{4,3,2,0,1:T(8,128)S(1)}, f32[2,2,5,18,256]{4,3,2,0,1:T(8,128)S(1)}, u32[]{:S(2)}, u32[]{:S(2)}) %collective-permute-start) | collective-permute-done | bytes 368672 | tf_op jit(solution)/shard_map/while/body/eval_jaxpr/ppermute | solution.py:29
  27.5 0.2 fusion.35
  27.8 0.3 subtract_reduce_fusion.3
  28.4 0.6 %gather_fusion = f32[4,2,3,16,256]{4,3,2,1,0:T(8,128)S(1)} fusion(f32[4,2,3,16,256]{4,3,2,1,0:T(8,128)S(1)} %pad_maximum_fusion.14, s32[1024]{0:T(1024)S(1)} %pad_clamp_fusion.3), kind=kCustom, calls=%fused_computation.clone.1 | custom fusion | bytes 786448 | tf_op jit(solution)/shard_map/while/body/eval_jaxpr/gather | solution.py:98
  29.0 7.5 %collective-permute-done = f32[2,2,5,18,256]{4,3,2,0,1:T(8,128)S(1)} collective-permute-done((f32[2,2,5,18,256]{4,3,2,0,1:T(8,128)S(1)}, f32[2,2,5,18,256]{4,3,2,0,1:T(8,128)S(1)}, u32[]{:S(2)}, u32[]{:S(2)}) %collective-permute-start) | collective-permute-done | bytes 368672 | tf_op jit(solution)/shard_map/while/body/eval_jaxpr/ppermute | solution.py:29
  36.9 0.2 fusion.35
  37.2 0.3 subtract_reduce_fusion.3
  37.8 0.6 %gather_fusion = f32[4,2,3,16,256]{4,3,2,1,0:T(8,128)S(1)} fusion(f32[4,2,3,16,256]{4,3,2,1,0:T(8,128)S(1)} %pad_maximum_fusion.14, s32[1024]{0:T(1024)S(1)} %pad_clamp_fusion.3), kind=kCustom, calls=%fused_computation.clone.1 | custom fusion | bytes 786448 | tf_op jit(solution)/shard_map/while/body/eval_jaxpr/gather | solution.py:98
  38.4 7.5 %collective-permute-done = f32[2,2,5,18,256]{4,3,2,0,1:T(8,128)S(1)} collective-permute-done((f32[2,2,5,18,256]{4,3,2,0,1:T(8,128)S(1)}, f32[2,2,5,18,256]{4,3,2,0,1:T(8,128)S(1)}, u32[]{:S(2)}, u32[]{:S(2)}) %collective-permute-start) | collective-permute-done | bytes 368672 | tf_op jit(solution)/shard_map/while/body/eval_jaxpr/ppermute | solution.py:29
  46.3 0.2 fusion.35
  46.5 0.3 subtract_reduce_fusion.3
  47.0 0.7 %copy.19 = f32[2,2,5,16,256]{4,3,2,1,0:T(8,128)} copy(f32[2,2,5,16,256]{4,3,2,0,1:T(8,128)S(1)} %get-tuple-element.231) | data formatting | bytes 655360 | tf_op jit(solution)/shard_map/while | solution.py:166
  (64 shorter events, 2.9 us)
Async XLA Ops:
  0.0 6.2 %copy-start.1 = (f32[16,256]{1,0:T(8,128)S(1)}, f32[16,256]{1,0:T(8,128)}, u32[]{:S(2)}) copy-start(f32[16,256]{1,0:T(8,128)} %param.11) | copy-start | bytes 49156
  0.0 6.4 %copy-start.2 = (f32[2,2,3,16,256]{4,3,2,1,0:T(8,128)S(1)}, f32[2,2,3,16,256]{4,3,2,1,0:T(8,128)}, u32[]{:S(2)}) copy-start(f32[2,2,3,16,256]{4,3,2,1,0:T(8,128)} %param.10) | copy-start | bytes 589828
  1.1 15.2 %collective-permute-start.2 = (f32[21,1,256]{2,1,0:T(1,128)S(1)}, f32[21,1,256]{2,1,0:T(1,128)S(1)}, u32[]{:S(2)}, u32[]{:S(2)}) collective-permute-start(f32[21,1,256]{2,1,0:T(1,128)S(1)} %get-tuple-element.304), channel_id=1, source_target_pairs={{1,0},{2,1},{3,2},{0,3},{5,4},{6,5},{7,6},{4,7},{9,8},{10,9},{11,1... | collective-permute-start | bytes 64520 | tf_op jit(solution)/shard_map/ppermute | solution.py:19
  6.2 10.1 %collective-permute-start.1 = (f32[21,1,256]{2,1,0:T(1,128)S(1)}, f32[21,1,256]{2,1,0:T(1,128)S(1)}, u32[]{:S(2)}, u32[]{:S(2)}) collective-permute-start(f32[21,1,256]{2,1,0:T(1,128)S(1)} %get-tuple-element.303), channel_id=1, source_target_pairs={{0,1},{1,2},{2,3},{3,0},{4,5},{5,6},{6,7},{7,4},{8,9},{9,10},{10,1... | collective-permute-start | bytes 64520 | tf_op jit(solution)/shard_map/ppermute | solution.py:17
  15.0 0.7 %copy-start.3 = (s32[4]{0:T(128)S(1)}, s32[4]{0:T(128)}, u32[]{:S(2)}) copy-start(s32[4]{0:T(128)} %constant.163) | copy-start | bytes 52
  16.3 1.0 %copy-start = (f32[2,2,5,16,256]{4,3,2,1,0:T(8,128)S(1)}, f32[2,2,5,16,256]{4,3,2,1,0:T(8,128)}, u32[]{:S(2)}) copy-start(f32[2,2,5,16,256]{4,3,2,1,0:T(8,128)} %param.9) | copy-start | bytes 983044
  18.8 8.3 %collective-permute-start = (f32[2,2,5,18,256]{4,3,2,0,1:T(8,128)S(1)}, f32[2,2,5,18,256]{4,3,2,0,1:T(8,128)S(1)}, u32[]{:S(2)}, u32[]{:S(2)}) collective-permute-start(f32[2,2,5,18,256]{4,3,2,0,1:T(8,128)S(1)} %get-tuple-element.397), channel_id=1, source_target_pairs={{0,4},{4,8},{8,12},{12,0},{1,5},{5,9},{9,13},{13,1},{2,6},{6,10},{... | collective-permute-start | bytes 1105928 | tf_op jit(solution)/shard_map/while/body/eval_jaxpr/ppermute | solution.py:29
  28.2 8.3 %collective-permute-start = (f32[2,2,5,18,256]{4,3,2,0,1:T(8,128)S(1)}, f32[2,2,5,18,256]{4,3,2,0,1:T(8,128)S(1)}, u32[]{:S(2)}, u32[]{:S(2)}) collective-permute-start(f32[2,2,5,18,256]{4,3,2,0,1:T(8,128)S(1)} %get-tuple-element.397), channel_id=1, source_target_pairs={{0,4},{4,8},{8,12},{12,0},{1,5},{5,9},{9,13},{13,1},{2,6},{6,10},{... | collective-permute-start | bytes 1105928 | tf_op jit(solution)/shard_map/while/body/eval_jaxpr/ppermute | solution.py:29
  37.6 8.3 %collective-permute-start = (f32[2,2,5,18,256]{4,3,2,0,1:T(8,128)S(1)}, f32[2,2,5,18,256]{4,3,2,0,1:T(8,128)S(1)}, u32[]{:S(2)}, u32[]{:S(2)}) collective-permute-start(f32[2,2,5,18,256]{4,3,2,0,1:T(8,128)S(1)} %get-tuple-element.397), channel_id=1, source_target_pairs={{0,4},{4,8},{8,12},{12,0},{1,5},{5,9},{9,13},{13,1},{2,6},{6,10},{... | collective-permute-start | bytes 1105928 | tf_op jit(solution)/shard_map/while/body/eval_jaxpr/ppermute | solution.py:29
where the time goes:
time: 47.9 us; the launch traced here: 47.7 us
  waiting for transfers between devices  22.2 us (46%)
  blocking collectives  8.61 us (18%)
  local copies, waits for them, and re-layouts  6.52 us (14%)
  starting transfers between devices  5.65 us (12%)
  other arithmetic  4.13 us (9%)
    ppermute x3, waiting for transfers between devices, shifted(): return lax.ppermute(value, axis, pairs)  22.2 us
    all_gather x1, blocking collectives, shards(): whole_base = lax.all_gather(base_flow, 'harm', axis=0, tiled=True)  8.61 us
    ppermute x1, starting transfers between devices, extended(): lax.ppermute(head, axis, [((i + 1) % count, i) for i in range(count)])  5.13 us
    gather x4, local copies, waits for them, and re-layouts, block_terms(): chosen = blocks[index_table]  2.3 us
    unnamed x11, local copies, waits for them, and re-layouts  1.54 us
    reduce_sum x4, other arithmetic, block_terms(): jnp.sum(real_part, axis=1)  1.12 us
    slice x1, other arithmetic, extended(): lax.slice_in_dim(cells, cells.shape[dim] - width, cells.shape[dim], axis=...  1.1 us
    slice x8, local copies, waits for them, and re-layouts, split_rows(): grad_y = 0.5 * (jnp.roll(middle, -1, -1) - jnp.roll(middle, 1, -1))  1.09 us
  transfers between devices with their start and end apart: 5, of which 3 were waited for; matrix products, arithmetic and copies ran while one was open for 6% of the time, Pallas kernels for 0%

commit v1 on v0

--- a/solution.py
+++ b/solution.py
@@ -137,7 +137,12 @@
     frequency = (omega_base * signed.astype(jnp.float32)).reshape(local_count, 1, 1, 1)
     middle, grad_x, grad_y = split_rows(own_padded)
     summed = own_terms(middle, grad_x, grad_y, diffusion(own_padded, visc_padded), frequency)
-    whole_base = lax.all_gather(base_flow, "harm", axis=0, tiled=True)
+    ring = [base_flow]
+    for hop in range(3):
+        ring.append(lax.ppermute(ring[-1], "harm", [(dev, (dev + 1) % 4) for dev in range(4)]))
+    whole_base = jnp.roll(
+        jnp.concatenate(ring[::-1], axis=0), (lax.axis_index("harm") + 1) * ring[0].shape[0], axis=0
+    )
 
     def base_pair(position, earlier):
         before = lax.dynamic_slice_in_dim(

time: 47.9 us -> 58.8 us (1.23)
  waiting for transfers between devices: 22.2 us -> 32 us
  blocking collectives: 8.61 us -> 0 us
  local copies, waits for them, and re-layouts: 6.52 us -> 11.6 us
  other arithmetic: 4.13 us -> 7.72 us
  starting transfers between devices: 5.65 us -> 6.56 us
    ppermute x0 -> x3, waiting for transfers between devices: none -> 8.72 us  [shards(): lax.ppermute(ring[-1], 'harm', [(dev, (dev + 1) % 4) for dev in range(4)])]
    all_gather x1 -> x0, blocking collectives: 8.61 us -> none  [shards(): whole_base = lax.all_gather(base_flow, 'harm', axis=0, tiled=True)]
    ppermute x1, starting transfers between devices: 5.13 us -> 2.09 us  [extended(): lax.ppermute(head, axis, [((i + 1) % count, i) for i in range(count)])]
    ppermute x1, starting transfers between devices: 0.01 us -> 2.62 us  [extended(): lax.ppermute(tail, axis, [(i, (i + 1) % count) for i in range(count)])]
    while x3, local copies, waits for them, and re-layouts: 0.1 us -> 2.35 us
    ppermute x0 -> x3, starting transfers between devices: none -> 1.85 us  [shards(): lax.ppermute(ring[-1], 'harm', [(dev, (dev + 1) % 4) for dev in range(4)])]
    slice x2, local copies, waits for them, and re-layouts: 0.14 us -> 1.65 us  [diffusion(): north_face = 0.5 * (center + jnp.roll(center, -1, -1))]
    reduce_sum x4, other arithmetic: 1.12 us -> 2.47 us  [block_terms(): jnp.sum(real_part, axis=1)]
  transfers between devices with their start and end apart: 5 -> 8, of which waited for: 3 -> 5; matrix products, arithmetic and copies ran while one was open for 6% -> 17% of each run, Pallas kernels for 0% -> 0%
where the time goes in v1:
time: 58.8 us; the launch traced here: 58.4 us
  waiting for transfers between devices  32 us (54%)
  local copies, waits for them, and re-layouts  11.6 us (20%)
  other arithmetic  7.72 us (13%)
  starting transfers between devices  6.56 us (11%)
    ppermute x3, waiting for transfers between devices, shifted(): return lax.ppermute(value, axis, pairs)  23.3 us
    ppermute x3, waiting for transfers between devices, shards(): lax.ppermute(ring[-1], 'harm', [(dev, (dev + 1) % 4) for dev in range(4)])  8.72 us
    ppermute x1, starting transfers between devices, extended(): lax.ppermute(tail, axis, [(i, (i + 1) % count) for i in range(count)])  2.62 us
    reduce_sum x4, other arithmetic, block_terms(): jnp.sum(real_part, axis=1)  2.47 us
    while x3, local copies, waits for them, and re-layouts  2.35 us
    gather x4, local copies, waits for them, and re-layouts, block_terms(): chosen = blocks[index_table]  2.3 us
    ppermute x1, starting transfers between devices, extended(): lax.ppermute(head, axis, [((i + 1) % count, i) for i in range(count)])  2.09 us
    ppermute x3, starting transfers between devices, shards(): lax.ppermute(ring[-1], 'harm', [(dev, (dev + 1) % 4) for dev in range(4)])  1.85 us
  transfers between devices with their start and end apart: 8, of which 5 were waited for; matrix products, arithmetic and copies ran while one was open for 17% of the time, Pallas kernels for 0%

profile of v1, /device:TPU:0, one launch (start us, length us, event | category | flops | bytes accessed | tf_op | source)
XLA Modules:
  0.0 58.4 jit_solution(6662371607162141685)
XLA Ops:
  0.5 1.1 %pad_maximum_fusion.8 = (f32[21,1,256]{2,1,0:T(1,128)S(1)}, f32[21,1,256]{2,1,0:T(1,128)S(1)}) fusion(f32[1,16,256]{2,1,0:T(8,128)} %bitcast.94, f32[20,16,256]{2,1,0:T(8,128)} %bitcast.90), kind=kLoop, calls=%fused_computation.67 | loop fusion | flops 10752 | bytes 387072 | tf_op jit(solution)/shard_map/slice | solution.py:14
  1.6 2.6 %collective-permute-start.1 = (f32[21,1,256]{2,1,0:T(1,128)S(1)}, f32[21,1,256]{2,1,0:T(1,128)S(1)}, u32[]{:S(2)}, u32[]{:S(2)}) collective-permute-start(f32[21,1,256]{2,1,0:T(1,128)S(1)} %get-tuple-element.303), channel_id=1, source_target_pairs={{0,1},{1,2},{2,3},{3,0},{4,5},{5,6},{6,7},{7,4},{8,9},{9,10},{10,1... | collective-permute-start | bytes 64520 | tf_op jit(solution)/shard_map/ppermute | solution.py:17
  4.2 2.1 %collective-permute-start.2 = (f32[21,1,256]{2,1,0:T(1,128)S(1)}, f32[21,1,256]{2,1,0:T(1,128)S(1)}, u32[]{:S(2)}, u32[]{:S(2)}) collective-permute-start(f32[21,1,256]{2,1,0:T(1,128)S(1)} %get-tuple-element.304), channel_id=1, source_target_pairs={{1,0},{2,1},{3,2},{0,3},{5,4},{6,5},{7,6},{4,7},{9,8},{10,9},{11,1... | collective-permute-start | bytes 64520 | tf_op jit(solution)/shard_map/ppermute | solution.py:19
  6.3 0.9 %fusion.19 = (f32[16,255]{1,0:T(8,128)S(1)}, f32[16,255]{1,0:T(8,128)S(1)}) fusion(f32[16,256]{1,0:T(8,128)} %param.11), kind=kLoop, calls=%fused_computation.94 | loop fusion | bytes 65280 | tf_op jit(solution)/shard_map/jit(_roll_static)/slice | solution.py:44
  7.1 0.8 %fusion.20 = (f32[16,1]{1,0:T(8,128)S(1)}, f32[16,1]{1,0:T(8,128)S(1)}) fusion(f32[16,256]{1,0:T(8,128)} %param.11), kind=kLoop, calls=%fused_computation.95 | loop fusion | bytes 256 | tf_op jit(solution)/shard_map/jit(_roll_static)/slice | solution.py:44
  7.9 0.7 %pad_clamp_fusion.1 = s32[1024]{0:T(1024)S(1)} fusion(s32[4]{0:T(128)} %constant.185), kind=kLoop, calls=%fused_computation.82 | loop fusion | flops 1024 | bytes 4112 | tf_op jit(solution)/shard_map/gather | solution.py:98
  8.6 1.1 %pad_maximum_fusion.1 = f32[20,18,256]{2,1,0:T(8,128)S(1)} fusion(f32[21,1,256]{2,1,0:T(1,128)S(1)} %collective-permute-done.2, f32[21,1,256]{2,1,0:T(1,128)S(1)} %collective-permute-done.1, f32[1,16,256]{2,1,0:T(8,128)} %bitcast.95, f32[20,16,256]{2,1,0:T(8,128)} %bitcast.91), kind=kLoop, calls=%fused_computation.25 | loop fusion | flops 276480 | bytes 755712 | tf_op jit(solution)/shard_map/concatenate | solution.py:15
  10.0 0.8 %copy.9 = f32[2,2,5,18,256]{4,3,2,0,1:T(8,128)} copy(f32[2,2,5,18,256]{4,3,2,1,0:T(8,128)S(1)} %bitcast.84) | data formatting | bytes 737280 | tf_op jit(solution)/shard_map/reshape | solution.py:132
  11.0 0.8 %slice_bitcast_fusion.15 = (f32[2,5,16,256]{3,2,1,0:T(8,128)}, f32[2,5,16,256]{3,2,1,0:T(8,128)}) fusion(f32[2,2,5,16,256]{4,3,2,0,1:T(8,128)S(1)} %get-tuple-element.316), kind=kLoop, calls=%fused_computation.41 | loop fusion | bytes 655360 | tf_op jit(solution)/shard_map/mul | solution.py:71
  11.8 0.8 %slice_bitcast_fusion.16 = (f32[2,5,16,256]{3,2,1,0:T(8,128)}, f32[2,5,16,256]{3,2,1,0:T(8,128)}, f32[2,1,5,16,256]{4,3,2,0,1:T(8,128)S(1)}, f32[2,1,5,16,256]{4,3,2,0,1:T(8,128)S(1)}) fusion(f32[2]{0:T(128)S(1)} %get-tuple-element.317, f32[2]{0:T(128)S(1)} %get-tuple-element.318, f32[2,2,5,18,256]{4,3,2,1,0:T(8,128)S(1)} %bitcast.86), kind=kLoop, calls=%fused_computation.42 | loop fusion | flops 81920 | bytes 984064 | tf_op jit(solution)/shard_map/mul | solution.py:75
  12.6 0.8 %slice_bitcast_fusion.13 = (f32[2,5,16,256]{3,2,1,0:T(8,128)}, f32[2,5,16,256]{3,2,1,0:T(8,128)}) fusion(f32[2,2,5,16,256]{4,3,2,0,1:T(8,128)S(1)} %get-tuple-element.315), kind=kLoop, calls=%fused_computation.39 | loop fusion | bytes 655360 | tf_op jit(solution)/shard_map/mul | solution.py:73
  13.4 1.4 %collective-permute-start.4 = (f32[2,2,3,16,256]{4,3,2,1,0:T(8,128)S(1)}, f32[2,2,3,16,256]{4,3,2,1,0:T(8,128)S(1)}, u32[]{:S(2)}, u32[]{:S(2)}) collective-permute-start(f32[2,2,3,16,256]{4,3,2,1,0:T(8,128)S(1)} %collective-permute-done.3), channel_id=1, source_target_pairs={{0,4},{4,8},{8,12},{12,0},{1,5},{5,9},{9,13},{13,1},{2,6},{6,10},{... | collective-permute-start | bytes 589832 | tf_op jit(solution)/shard_map/ppermute | solution.py:142
  14.8 3.7 %collective-permute-done.4 = f32[2,2,3,16,256]{4,3,2,1,0:T(8,128)S(1)} collective-permute-done((f32[2,2,3,16,256]{4,3,2,1,0:T(8,128)S(1)}, f32[2,2,3,16,256]{4,3,2,1,0:T(8,128)S(1)}, u32[]{:S(2)}, u32[]{:S(2)}) %collective-permute-start.4) | collective-permute-done | bytes 196640 | tf_op jit(solution)/shard_map/ppermute | solution.py:142
  18.6 5.0 %collective-permute-done.5 = f32[2,2,3,16,256]{4,3,2,1,0:T(8,128)S(1)} collective-permute-done((f32[2,2,3,16,256]{4,3,2,1,0:T(8,128)S(1)}, f32[2,2,3,16,256]{4,3,2,1,0:T(8,128)S(1)}, u32[]{:S(2)}, u32[]{:S(2)}) %collective-permute-start.5) | collective-permute-done | bytes 196640 | tf_op jit(solution)/shard_map/ppermute | solution.py:142
  23.9 0.6 gather_fusion.1
  24.5 1.6 %subtract_reduce_fusion.1 = (f32[2,5,16,256]{3,2,1,0:T(8,128)S(1)}, f32[2,5,16,256]{3,2,1,0:T(8,128)S(1)}) fusion(f32[2,5,16,256]{3,2,1,0:T(8,128)} %get-tuple-element.288, f32[2,2,16,256]{3,2,1,0:T(8,128)S(1)} %get-tuple-element.300, f32[2,5,16,256]{3,2,1,0:T(8,128)} %get-tuple-element.287, f32[2,2,16,256]{3,2,1,0:T(8,128)S(1)} %get-tuple-element.296, ...), kind=kLoop, calls=%fused_computation.35 | loop fusion | flops 1884160 | bytes 1703936 | tf_op jit(solution)/shard_map/reduce_sum | solution.py:120
  26.8 30.8 %while.21 = (s32[]{:T(128)}, f32[2,2,5,16,256]{4,3,2,0,1:T(8,128)S(1)}, f32[2,2,5,18,256]{4,3,2,0,1:T(8,128)}, f32[8,2,3,16,256]{4,3,2,1,0:T(8,128)S(1)}, s32[]{...) while((s32[]{:T(128)}, ...), condition=%wide.region_5.6_spmd.clone, body=%wide.region_2.5_spmd.sunk.clone.sunk | while | flops 2638870 | bytes 13291922 | solution.py:171
  27.6 7.8 %collective-permute-done = f32[2,2,5,18,256]{4,3,2,0,1:T(8,128)S(1)} collective-permute-done((f32[2,2,5,18,256]{4,3,2,0,1:T(8,128)}, f32[2,2,5,18,256]{4,3,2,0,1:T(8,128)S(1)}, u32[]{:S(2)}, u32[]{:S(2)}) %collective-permute-start) | collective-permute-done | bytes 368672 | tf_op jit(solution)/shard_map/while/body/eval_jaxpr/ppermute | solution.py:29
  36.3 0.8 %copy.49 = f32[2,2,5,18,256]{4,3,2,0,1:T(8,128)} copy(f32[2,2,5,18,256]{4,3,2,0,1:T(8,128)S(1)} %collective-permute-done) | data formatting | bytes 737280 | tf_op jit(solution)/shard_map/while
  37.8 7.8 %collective-permute-done = f32[2,2,5,18,256]{4,3,2,0,1:T(8,128)S(1)} collective-permute-done((f32[2,2,5,18,256]{4,3,2,0,1:T(8,128)}, f32[2,2,5,18,256]{4,3,2,0,1:T(8,128)S(1)}, u32[]{:S(2)}, u32[]{:S(2)}) %collective-permute-start) | collective-permute-done | bytes 368672 | tf_op jit(solution)/shard_map/while/body/eval_jaxpr/ppermute | solution.py:29
  46.6 0.8 %copy.49 = f32[2,2,5,18,256]{4,3,2,0,1:T(8,128)} copy(f32[2,2,5,18,256]{4,3,2,0,1:T(8,128)S(1)} %collective-permute-done) | data formatting | bytes 737280 | tf_op jit(solution)/shard_map/while
  48.1 7.8 %collective-permute-done = f32[2,2,5,18,256]{4,3,2,0,1:T(8,128)S(1)} collective-permute-done((f32[2,2,5,18,256]{4,3,2,0,1:T(8,128)}, f32[2,2,5,18,256]{4,3,2,0,1:T(8,128)S(1)}, u32[]{:S(2)}, u32[]{:S(2)}) %collective-permute-start) | collective-permute-done | bytes 368672 | tf_op jit(solution)/shard_map/while/body/eval_jaxpr/ppermute | solution.py:29
  56.9 0.8 %copy.49 = f32[2,2,5,18,256]{4,3,2,0,1:T(8,128)} copy(f32[2,2,5,18,256]{4,3,2,0,1:T(8,128)S(1)} %collective-permute-done) | data formatting | bytes 737280 | tf_op jit(solution)/shard_map/while
  57.7 0.7 %copy.19 = f32[2,2,5,16,256]{4,3,2,1,0:T(8,128)} copy(f32[2,2,5,16,256]{4,3,2,0,1:T(8,128)S(1)} %get-tuple-element.231) | data formatting | bytes 655360 | tf_op jit(solution)/shard_map/while | solution.py:171
  (82 shorter events, 7.0 us)
Async XLA Ops:
  0.0 13.4 %collective-permute-start.3 = (f32[2,2,3,16,256]{4,3,2,1,0:T(8,128)}, f32[2,2,3,16,256]{4,3,2,1,0:T(8,128)S(1)}, u32[]{:S(2)}, u32[]{:S(2)}) collective-permute-start(f32[2,2,3,16,256]{4,3,2,1,0:T(8,128)} %param.10), channel_id=1, source_target_pairs={{0,4},{4,8},{8,12},{12,0},{1,5},{5,9},{9,13},{13,1},{2,6},{6,10},{... | collective-permute-start | bytes 589832 | tf_op jit(solution)/shard_map/ppermute | solution.py:142
  1.6 7.0 %collective-permute-start.1 = (f32[21,1,256]{2,1,0:T(1,128)S(1)}, f32[21,1,256]{2,1,0:T(1,128)S(1)}, u32[]{:S(2)}, u32[]{:S(2)}) collective-permute-start(f32[21,1,256]{2,1,0:T(1,128)S(1)} %get-tuple-element.303), channel_id=1, source_target_pairs={{0,1},{1,2},{2,3},{3,0},{4,5},{5,6},{6,7},{7,4},{8,9},{9,10},{10,1... | collective-permute-start | bytes 64520 | tf_op jit(solution)/shard_map/ppermute | solution.py:17
  4.2 4.4 %collective-permute-start.2 = (f32[21,1,256]{2,1,0:T(1,128)S(1)}, f32[21,1,256]{2,1,0:T(1,128)S(1)}, u32[]{:S(2)}, u32[]{:S(2)}) collective-permute-start(f32[21,1,256]{2,1,0:T(1,128)S(1)} %get-tuple-element.304), channel_id=1, source_target_pairs={{1,0},{2,1},{3,2},{0,3},{5,4},{6,5},{7,6},{4,7},{9,8},{10,9},{11,1... | collective-permute-start | bytes 64520 | tf_op jit(solution)/shard_map/ppermute | solution.py:19
  11.0 7.5 %copy-start = (f32[2,2,5,16,256]{4,3,2,1,0:T(8,128)S(1)}, f32[2,2,5,16,256]{4,3,2,1,0:T(8,128)}, u32[]{:S(2)}) copy-start(f32[2,2,5,16,256]{4,3,2,1,0:T(8,128)} %param.9) | copy-start | bytes 983044
  11.0 7.5 %copy-start.1 = (f32[16,256]{1,0:T(8,128)S(1)}, f32[16,256]{1,0:T(8,128)}, u32[]{:S(2)}) copy-start(f32[16,256]{1,0:T(8,128)} %param.11) | copy-start | bytes 49156
  11.8 11.8 %copy-start.2 = (f32[2,2,3,16,256]{4,3,2,1,0:T(8,128)S(1)}, f32[2,2,3,16,256]{4,3,2,1,0:T(8,128)}, u32[]{:S(2)}) copy-start(f32[2,2,3,16,256]{4,3,2,1,0:T(8,128)} %param.10) | copy-start | bytes 589828
  13.4 5.1 %collective-permute-start.4 = (f32[2,2,3,16,256]{4,3,2,1,0:T(8,128)S(1)}, f32[2,2,3,16,256]{4,3,2,1,0:T(8,128)S(1)}, u32[]{:S(2)}, u32[]{:S(2)}) collective-permute-start(f32[2,2,3,16,256]{4,3,2,1,0:T(8,128)S(1)} %collective-permute-done.3), channel_id=1, source_target_pairs={{0,4},{4,8},{8,12},{12,0},{1,5},{5,9},{9,13},{13,1},{2,6},{6,10},{... | collective-permute-start | bytes 589832 | tf_op jit(solution)/shard_map/ppermute | solution.py:142
  14.7 9.0 %copy-start.3 = (f32[2,2,5,16,256]{4,3,2,0,1:T(8,128)}, f32[2,2,5,16,256]{4,3,2,0,1:T(8,128)S(1)}, u32[]{:S(2)}) copy-start(f32[2,2,5,16,256]{4,3,2,0,1:T(8,128)S(1)} %constant_dynamic-update-slice_fusion) | copy-start | bytes 983044
  18.5 5.1 %collective-permute-start.5 = (f32[2,2,3,16,256]{4,3,2,1,0:T(8,128)S(1)}, f32[2,2,3,16,256]{4,3,2,1,0:T(8,128)S(1)}, u32[]{:S(2)}, u32[]{:S(2)}) collective-permute-start(f32[2,2,3,16,256]{4,3,2,1,0:T(8,128)S(1)} %collective-permute-done.4), channel_id=1, source_target_pairs={{0,4},{4,8},{8,12},{12,0},{1,5},{5,9},{9,13},{13,1},{2,6},{6,10},{... | collective-permute-start | bytes 589832 | tf_op jit(solution)/shard_map/ppermute | solution.py:142
  24.5 1.7 %copy-start.4 = (f32[2,2,5,16,256]{4,3,2,0,1:T(8,128)S(1)}, f32[2,2,5,16,256]{4,3,2,0,1:T(8,128)}, u32[]{:S(2)}) copy-start(f32[2,2,5,16,256]{4,3,2,0,1:T(8,128)} %copy-done.3) | copy-start | bytes 983044
  26.2 0.7 %copy-start.5 = (s32[4]{0:T(128)S(1)}, s32[4]{0:T(128)}, u32[]{:S(2)}) copy-start(s32[4]{0:T(128)} %constant.185) | copy-start | bytes 52
  26.9 8.5 %collective-permute-start = (f32[2,2,5,18,256]{4,3,2,0,1:T(8,128)}, f32[2,2,5,18,256]{4,3,2,0,1:T(8,128)S(1)}, u32[]{:S(2)}, u32[]{:S(2)}) collective-permute-start(f32[2,2,5,18,256]{4,3,2,0,1:T(8,128)} %get-tuple-element.397), channel_id=1, source_target_pairs={{0,4},{4,8},{8,12},{12,0},{1,5},{5,9},{9,13},{13,1},{2,6},{6,10},{... | collective-permute-start | bytes 1105928 | tf_op jit(solution)/shard_map/while/body/eval_jaxpr/ppermute | solution.py:29
  37.1 8.5 %collective-permute-start = (f32[2,2,5,18,256]{4,3,2,0,1:T(8,128)}, f32[2,2,5,18,256]{4,3,2,0,1:T(8,128)S(1)}, u32[]{:S(2)}, u32[]{:S(2)}) collective-permute-start(f32[2,2,5,18,256]{4,3,2,0,1:T(8,128)} %get-tuple-element.397), channel_id=1, source_target_pairs={{0,4},{4,8},{8,12},{12,0},{1,5},{5,9},{9,13},{13,1},{2,6},{6,10},{... | collective-permute-start | bytes 1105928 | tf_op jit(solution)/shard_map/while/body/eval_jaxpr/ppermute | solution.py:29
  47.4 8.5 %collective-permute-start = (f32[2,2,5,18,256]{4,3,2,0,1:T(8,128)}, f32[2,2,5,18,256]{4,3,2,0,1:T(8,128)S(1)}, u32[]{:S(2)}, u32[]{:S(2)}) collective-permute-start(f32[2,2,5,18,256]{4,3,2,0,1:T(8,128)} %get-tuple-element.397), channel_id=1, source_target_pairs={{0,4},{4,8},{8,12},{12,0},{1,5},{5,9},{9,13},{13,1},{2,6},{6,10},{... | collective-permute-start | bytes 1105928 | tf_op jit(solution)/shard_map/while/body/eval_jaxpr/ppermute | solution.py:29
